TPU v7x, 256 devices: a whole 4x4x8 slice. The times are simulated.
256 devices in a mesh: lat: 32 (over z, x), lev: 8 (over y, core).
Axes of the slice: x: 4, y: 4, z: 8, core: 2. Of those that a mesh axis runs over, the one named last changes fastest.
Arguments:
- tokens: bfloat16 [2, 8, 64, 64, 1024], P(None, 'lev', 'lat'), may hold values from -40 to 40
- key_mask: int32 [2, 64], replicated, may hold values from 0 to 1, as said below
- w_qkv: bfloat16 [1024, 3072], replicated, may hold values from -0.1875 to 0.1875
- w_mix: bfloat16 [8, 1024, 1024], P('lev'), may hold values from -0.0625 to 0.0625
- level_scale: float32 [8, 1024], P('lev'), may hold values from 0.1 to 1.9
- cotangent: bfloat16 [2, 8, 64, 64, 1024], P(None, 'lev', 'lat'), may hold values from -6 to 6
Outputs:
- output: bfloat16 [2, 8, 64, 64, 1024], P(None, 'lev', 'lat')
- d_tokens: bfloat16 [2, 8, 64, 64, 1024], P(None, 'lev', 'lat')
- mix_grad: float32 [8, 1024, 1024], P('lev', 'lat')
Inputs may be any that keep to these rules, and one draw needn't show every extreme that they name: `key_mask`: each sample has 1 to 4 padded rows, all at the end of the latitude rows, and the rest real; some sample has exactly 4 padded rows.
All inputs are finite; a program needn't handle non-finite values.
Results may differ from a plain program's by a relative error of at most 0.015.
Values may be sent and summed in bfloat16 or wider, within the bound.
A program may use at most 128 MiB of HBM per device.

v0:
```python
import math

import jax
import jax.numpy as jnp
from jax import lax
from jax.sharding import PartitionSpec as P

HEADS = 16


epsilon = 1e-06
score_scale = 0.25


def rms_factor(values):
    return lax.rsqrt(jnp.mean(values * values, axis=-1, keepdims=True) + epsilon)


def norm_backward(values, factor, upstream):
    inner_mean = jnp.mean(upstream * values, axis=-1, keepdims=True)
    return factor * upstream - values * (factor * factor * factor) * inner_mean


def level_total(partial_value):
    return lax.psum(partial_value, "lev")


def to_columns(block):
    return lax.all_to_all(block, "lat", split_axis=2, concat_axis=1, tiled=True)


def to_bands(block):
    return lax.all_to_all(block, "lat", split_axis=1, concat_axis=2, tiled=True)


def column_weights(query_col, key_col, valid_keys):
    scores = (
        jnp.einsum("bligpe,blkgpe->blgpik", query_col, key_col, preferred_element_type=jnp.float32)
        * score_scale
    )
    exp_scores = jnp.exp(scores) * valid_keys.astype(jnp.float32)[:, None, None, None, None, :]
    return exp_scores / jnp.sum(exp_scores, axis=-1, keepdims=True)


def on_device(tokens, key_mask, w_qkv, w_mix, level_scale, cotangent):
    batch_count, level_local, band_rows, lon_cells, model_width = tokens.shape
    head_width = model_width // HEADS
    head_pairs = 128 // head_width
    column_groups = lon_cells * model_width // 128
    token_count = batch_count * level_local * band_rows * lon_cells
    item_count = batch_count * level_local
    tokens_f32 = tokens.astype(jnp.float32).reshape(token_count, model_width)
    factor = rms_factor(tokens_f32)
    normed = (tokens_f32 * factor).astype(jnp.bfloat16)
    w_split = w_qkv.reshape(model_width, 3, model_width)
    projected = jnp.einsum("rd,dce->cre", normed, w_split, preferred_element_type=jnp.float32)
    heads_view = projected.reshape(3, token_count, model_width // head_width, head_width)
    qk_raw = heads_view[:2]
    qk_factor = rms_factor(qk_raw)
    sent = jnp.concatenate(
        [(qk_raw * qk_factor).astype(jnp.bfloat16), heads_view[2:].astype(jnp.bfloat16)], axis=0
    )
    band_block = sent.reshape(3 * item_count, band_rows, column_groups, 128)
    column_block = to_columns(band_block)
    lat_all = column_block.shape[1]
    local_groups = column_block.shape[2]
    col_shape = (batch_count, level_local, lat_all, local_groups, head_pairs, head_width)
    stacked = column_block.reshape((3,) + col_shape)
    query_col, key_col, value_col = (stacked[0], stacked[1], stacked[2])
    weights = column_weights(query_col, key_col, key_mask)
    attended_col = jnp.einsum(
        "blgpik,blkgpe->bligpe",
        weights.astype(jnp.bfloat16),
        value_col,
        preferred_element_type=jnp.float32,
    ).astype(jnp.bfloat16)
    attended = to_bands(attended_col.reshape(item_count, lat_all, local_groups, 128))
    attended = attended.reshape(batch_count, level_local, band_rows * lon_cells, model_width)
    partial_value = jnp.einsum("blrd,lde->bre", attended, w_mix, preferred_element_type=jnp.float32)
    level_mix = level_total(partial_value)
    level_gain = level_scale[None, :, None, :]
    tokens_view = tokens_f32.reshape(batch_count, level_local, band_rows * lon_cells, model_width)
    output = (
        (tokens_view + level_gain * level_mix[:, None]).astype(jnp.bfloat16).reshape(tokens.shape)
    )
    cot_view = cotangent.astype(jnp.float32).reshape(
        batch_count, level_local, band_rows * lon_cells, model_width
    )
    flow_part = jnp.sum(level_gain * cot_view, axis=1)
    flow_b = level_total(flow_part).astype(jnp.bfloat16)
    token_total = batch_count * band_rows * lon_cells * lax.axis_size("lat")
    mix_term = jnp.einsum(
        "blrd,bre->lde", attended, flow_b, preferred_element_type=jnp.float32
    ) / math.sqrt(token_total)
    mix_grad = lax.psum_scatter(
        mix_term.astype(jnp.bfloat16), "lat", scatter_dimension=1, tiled=True
    ).astype(jnp.float32)
    d_attended = jnp.einsum(
        "bre,lde->blrd", flow_b, w_mix, preferred_element_type=jnp.float32
    ).astype(jnp.bfloat16)
    d_block = d_attended.reshape(item_count, band_rows, column_groups, 128)
    d_col = to_columns(d_block).reshape(col_shape)
    query_use, key_use, value_use = (query_col, key_col, value_col)
    d_value = jnp.einsum(
        "blgpik,bligpe->blkgpe",
        weights.astype(jnp.bfloat16),
        d_col,
        preferred_element_type=jnp.float32,
    ).astype(jnp.bfloat16)
    d_attn = jnp.einsum(
        "bligpe,blkgpe->blgpik", d_col, value_use, preferred_element_type=jnp.float32
    )
    d_scores = weights * (d_attn - jnp.sum(weights * d_attn, axis=-1, keepdims=True))
    d_scores_b = (d_scores * score_scale).astype(jnp.bfloat16)
    d_query = jnp.einsum(
        "blgpik,blkgpe->bligpe", d_scores_b, key_use, preferred_element_type=jnp.float32
    ).astype(jnp.bfloat16)
    d_key = jnp.einsum(
        "blgpik,bligpe->blkgpe", d_scores_b, query_use, preferred_element_type=jnp.float32
    ).astype(jnp.bfloat16)
    returned = to_bands(
        jnp.stack([d_query, d_key, d_value]).reshape(3 * item_count, lat_all, local_groups, 128)
    )
    returned = returned.reshape(3, token_count, model_width // head_width, head_width)
    grads_qk = norm_backward(qk_raw, qk_factor, returned[:2].astype(jnp.float32)).astype(
        jnp.bfloat16
    )
    grad_proj = jnp.concatenate([grads_qk, returned[2:]], axis=0).reshape(
        3, token_count, model_width
    )
    d_normed = jnp.einsum("cre,dce->rd", grad_proj, w_split, preferred_element_type=jnp.float32)
    cot_flat = cot_view.reshape(token_count, model_width)
    d_tokens = (
        (cot_flat + norm_backward(tokens_f32, factor, d_normed))
        .astype(jnp.bfloat16)
        .reshape(tokens.shape)
    )
    return (output, d_tokens, mix_grad)


def solution(mesh):
    return jax.shard_map(
        on_device,
        mesh=mesh,
        in_specs=(
            P(None, "lev", "lat", None, None),
            P(),
            P(),
            P("lev", None, None),
            P("lev", None),
            P(None, "lev", "lat", None, None),
        ),
        out_specs=(
            P(None, "lev", "lat", None, None),
            P(None, "lev", "lat", None, None),
            P("lev", "lat", None),
        ),
        check_vma=False,
    )
```

profile of v0, /device:TPU:1, one launch (start us, length us, event | category | flops | bytes accessed | tf_op | source)
XLA Modules:
  0.0 561.7 jit_solution(14300768743328919912)
XLA Ops:
  7.2 1.4 multiply_reduce_fusion.3
  8.6 1.2 multiply_convert_fusion.2
  9.8 8.6 %copy.92 = bf16[1024,3072]{0,1:T(8,128)(2,1)} copy(bf16[1024,3072]{1,0:T(8,128)(2,1)} %param.8) | data formatting | bytes 12582912 | tf_op args[2]
  18.4 4.6 convolution_bitcast_fusion
  23.1 1.7 copy-done.5
  24.8 1.5 slice.39
  26.4 2.9 copy.94
  29.4 2.0 multiply_reduce_fusion.2
  31.6 0.3 multiply_convert_fusion.1
  31.9 1.3 pad_maximum_fusion.1
  33.1 5.3 copy.96
  38.4 5.2 reshape.228
  43.6 4.2 copy.97
  47.8 12.1 %all-to-all-start = ((bf16[6,2,512,128]{3,1,0,2:T(2,128)(2,1)}), bf16[6,2,512,128]{3,1,0,2:T(2,128)(2,1)}, u32[]{:S(2)}, u32[]{:S(2)}) async-start(bf16[6,2,512,128]{3,1,0,2:T(2,128)(2,1)} %copy.97), calls=%async_computation | async-start | bytes 3145728 | tf_op jit(solution)/shard_map/all_to_all | solution.py:29
  59.9 0.2 all-reduce.3.cloned.1.call-start
  60.2 37.6 %all-to-all-done = bf16[6,2,512,128]{3,1,0,2:T(2,128)(2,1)} async-done(((bf16[6,2,512,128]{3,1,0,2:T(2,128)(2,1)}), bf16[6,2,512,128]{3,1,0,2:T(2,128)(2,1)}, u32[]{:S(2)}, u32[]{:S(2)}) %all-to-all-start) | async-done | bytes 1572896 | tf_op jit(solution)/shard_map/all_to_all | solution.py:29
  97.8 1.7 copy.98
  99.4 1.1 fusion.70
  100.6 1.5 reshape.229
  102.1 1.4 reshape.230
  103.4 2.8 copy.116
  106.2 2.3 copy.101
  108.5 3.2 reshape.231
  111.6 3.8 copy.114
  115.5 2.1 fusion.10
  117.6 1.8 convolution_convert_fusion.1
  119.4 2.0 copy.106
  121.4 20.6 %all_to_all.60 = bf16[2,64,16,128]{3,2,0,1:T(8,128)(2,1)S(1)} all-to-all(bf16[2,64,16,128]{3,2,0,1:T(8,128)(2,1)S(1)} %copy.106), channel_id=1, replica_groups=mesh['lat'=32,'lev'=8] {'lat'}, dimensions={1} | all-to-all | bytes 1048576 | tf_op jit(solution)/shard_map/all_to_all | solution.py:33
  142.0 0.2 reshape.233
  142.3 1.7 fusion.4
  144.0 65.4 %all-reduce.3.cloned.1.call-done = f32[2,128,1024]{2,1,0:T(8,128)} async-done(((f32[2,128,1024]{2,1,0:T(8,128)}), f32[2,128,1024]{2,1,0:T(8,128)}) %all-reduce.3.cloned.1.call-update) | async-done | bytes 1048592 | tf_op jit(solution)/shard_map/psum | solution.py:25
  209.5 2.8 bitcast_multiply_fusion.3
  212.3 52.7 %all-reduce.4 = bf16[2,128,1024]{2,1,0:T(8,128)(2,1)} all-reduce(f32[2,128,1024]{2,1,0:T(8,128)} %get-tuple-element.20), channel_id=1, replica_groups=mesh['lat'=32,'lev'=8] {'lev'}, use_global_device_ids=true, to_apply=%region_4.0 | all-reduce | flops 262144 | bytes 1572864 | tf_op jit(solution)/shard_map/psum | solution.py:25
  265.0 2.6 fusion.41
  267.5 1.3 reshape.237
  268.8 0.5 copy.109
  269.4 23.9 %all_to_all.61 = bf16[2,2,512,128]{3,1,0,2:T(2,128)(2,1)S(1)} all-to-all(bf16[2,2,512,128]{3,1,0,2:T(2,128)(2,1)S(1)} %copy.109), channel_id=1, replica_groups=mesh['lat'=32,'lev'=8] {'lat'}, dimensions={2} | all-to-all | bytes 1048576 | tf_op jit(solution)/shard_map/all_to_all | solution.py:29
  293.4 0.4 reshape.238
  293.8 2.2 copy.118
  296.1 3.8 fusion.28
  299.9 1.9 fusion.53
  301.8 5.9 %fusion.29 = bf16[1,2,1,64,16,2,64]{3,6,5,4,1,2,0:T(8,128)(2,1)} fusion(bf16[2,64,16,2,64]{1,4,3,2,0:T(8,128)(2,1)S(1)} %copy-done.7, f32[2,16,2,64,64]{3,4,2,1,0:T(8,128)} %fusion.53, f32[2,16,2,64,64]{3,4,2,1,0:T(8,128)} %copy-done.12, f32[2,16,2,64]{3,2,1,0:T(2,128)S(1)} %get-tuple-element.22, f32[2,64]{1,0:T(2,128)S(1)} %convert_element_type.127), kind=kOutput, calls=%fused_computation.32 | convolution fusion | flops 36704320 | bytes 3162624 | tf_op jit(solution)/shard_map/blgpik,bligpe->blkgpe/dot_general | solution.py:118
  307.7 6.1 %fusion.32 = bf16[1,2,1,64,16,2,64]{3,6,5,4,1,2,0:T(8,128)(2,1)} fusion(bf16[2,64,16,2,64]{1,4,3,2,0:T(8,128)(2,1)S(1)} %copy-done.8, f32[2,16,2,64,64]{3,4,2,1,0:T(8,128)} %fusion.53, f32[2,16,2,64,64]{3,4,2,1,0:T(8,128)} %copy-done.12, f32[2,16,2,64]{3,2,1,0:T(2,128)S(1)} %get-tuple-element.22, f32[2,64]{1,0:T(2,128)S(1)} %convert_element_type.127), kind=kOutput, calls=%fused_computation.33 | convolution fusion | flops 36704320 | bytes 3162624 | tf_op jit(solution)/shard_map/blgpik,blkgpe->bligpe/dot_general | solution.py:115
  313.8 4.0 pad_maximum_fusion
  317.8 4.9 copy.120
  322.7 6.4 %all-to-all-start.3 = ((bf16[6,64,16,128]{3,2,0,1:T(8,128)(2,1)}), bf16[6,64,16,128]{3,2,0,1:T(8,128)(2,1)}, u32[]{:S(2)}, u32[]{:S(2)}) async-start(bf16[6,64,16,128]{3,2,0,1:T(8,128)(2,1)} %copy.120), calls=%async_computation.3 | async-start | bytes 3145728 | tf_op jit(solution)/shard_map/all_to_all | solution.py:33
  329.2 0.3 reduce-scatter.2.cloned.1.call-start
  329.5 2.0 fusion.17
  331.8 1.8 copy.124
  333.8 1.8 copy.123
  335.6 30.3 %all-to-all-done.3 = bf16[6,64,16,128]{3,2,0,1:T(8,128)(2,1)} async-done(((bf16[6,64,16,128]{3,2,0,1:T(8,128)(2,1)}), bf16[6,64,16,128]{3,2,0,1:T(8,128)(2,1)}, u32[]{:S(2)}, u32[]{:S(2)}) %all-to-all-start.3) | async-done | bytes 1572896 | tf_op jit(solution)/shard_map/all_to_all | solution.py:33
  366.0 1.7 copy.121
  367.7 0.3 slice_convert_fusion
  368.2 2.4 reshape.243
  370.6 1.5 reshape.242
  372.1 0.2 concatenate.10
  372.4 4.8 copy.126
  377.2 2.0 multiply_reduce_fusion
  379.4 1.8 copy.127
  381.2 5.1 subtract_convert_fusion
  386.4 4.9 fusion.48
  391.3 1.1 fusion.47
  392.4 161.0 %reduce-scatter.2.cloned.1.call-done = bf16[1,32,1024]{2,1,0:T(8,128)(2,1)} async-done(((bf16[1,1024,1024]{2,1,0:T(8,128)(2,1)}), bf16[1,32,1024]{2,1,0:T(8,128)(2,1)}) %reduce-scatter.2.cloned.1.call-update) | async-done | bytes 65552 | tf_op jit(solution)/shard_map/reduce_scatter | solution.py:95
  553.4 1.5 convert_element_type.157
  (56 shorter events, 1.7 us)
Async XLA Ops:
  7.2 135.1 %copy-start = (bf16[1,1024,1024]{2,1,0:T(8,128)(2,1)S(1)}, bf16[1,1024,1024]{2,1,0:T(8,128)(2,1)}, u32[]{:S(2)}) copy-start(bf16[1,1024,1024]{2,1,0:T(8,128)(2,1)} %param.9) | copy-start | bytes 6291460
  23.0 1.7 copy-start.5
  29.4 2.2 copy-start.2
  47.8 12.3 %copy-start.17 = (s32[2,64]{1,0:T(2,128)S(1)}, s32[2,64]{1,0:T(2,128)}, u32[]{:S(2)}) copy-start(s32[2,64]{1,0:T(2,128)} %param.7) | copy-start | bytes 1540
  47.8 50.0 %all-to-all-start = ((bf16[6,2,512,128]{3,1,0,2:T(2,128)(2,1)}), bf16[6,2,512,128]{3,1,0,2:T(2,128)(2,1)}, u32[]{:S(2)}, u32[]{:S(2)}) async-start(bf16[6,2,512,128]{3,1,0,2:T(2,128)(2,1)} %copy.97), calls=%async_computation | async-start | bytes 3145728 | tf_op jit(solution)/shard_map/all_to_all | solution.py:29
  59.9 149.5 %all-reduce.3.cloned.1.call-start = ((), (), s32[]{:S(2)}) async-start(), calls=%async_computation.5 | async-start | bytes 2097152 | tf_op jit(solution)/shard_map/psum | solution.py:25
  106.2 9.3 %copy-start.6 = (bf16[2,64,16,2,64]{1,4,3,2,0:T(8,128)(2,1)}, bf16[2,64,16,2,64]{1,4,3,2,0:T(8,128)(2,1)S(1)}, u32[]{:S(2)}) copy-start(bf16[2,64,16,2,64]{1,4,3,2,0:T(8,128)(2,1)S(1)} %copy.116) | copy-start | bytes 1572868
  115.4 2.1 copy-start.9
  117.6 1.8 copy-start.12
  142.2 67.2 %copy-start.4 = (bf16[2,1,2,64,1024]{4,3,2,1,0:T(8,128)(2,1)S(1)}, bf16[2,1,2,64,1024]{4,3,2,1,0:T(8,128)(2,1)}, u32[]{:S(2)}) copy-start(bf16[2,1,2,64,1024]{4,3,2,1,0:T(8,128)(2,1)} %param.6) | copy-start | bytes 1572868
  142.3 67.2 %copy-start.16 = (f32[1,1024]{1,0:T(1,128)S(1)}, f32[1,1024]{1,0:T(1,128)}, u32[]{:S(2)}) copy-start(f32[1,1024]{1,0:T(1,128)} %param.10) | copy-start | bytes 12292
  296.1 3.8 copy-start.10
  296.1 3.8 copy-start.11
  299.9 1.9 copy-start.7
  301.8 5.9 %copy-start.8 = (bf16[2,64,16,2,64]{1,4,3,2,0:T(8,128)(2,1)S(1)}, bf16[2,64,16,2,64]{1,4,3,2,0:T(8,128)(2,1)}, u32[]{:S(2)}) copy-start(bf16[2,64,16,2,64]{1,4,3,2,0:T(8,128)(2,1)} %copy.114) | copy-start | bytes 1572868
  307.7 6.1 %copy-start.15 = (bf16[1,2,1,64,16,2,64]{3,6,5,4,1,2,0:T(8,128)(2,1)S(1)}, bf16[1,2,1,64,16,2,64]{3,6,5,4,1,2,0:T(8,128)(2,1)}, u32[]{:S(2)}) copy-start(bf16[1,2,1,64,16,2,64]{3,6,5,4,1,2,0:T(8,128)(2,1)} %fusion.28) | copy-start | bytes 1572868
  322.7 6.8 %copy-start.13 = (bf16[2,128,1024]{2,1,0:T(8,128)(2,1)S(1)}, bf16[2,128,1024]{2,1,0:T(8,128)(2,1)}, u32[]{:S(2)}) copy-start(bf16[2,128,1024]{2,1,0:T(8,128)(2,1)} %all-reduce.4) | copy-start | bytes 1572868
  322.7 43.3 %all-to-all-start.3 = ((bf16[6,64,16,128]{3,2,0,1:T(8,128)(2,1)}), bf16[6,64,16,128]{3,2,0,1:T(8,128)(2,1)}, u32[]{:S(2)}, u32[]{:S(2)}) async-start(bf16[6,64,16,128]{3,2,0,1:T(8,128)(2,1)} %copy.120), calls=%async_computation.3 | async-start | bytes 3145728 | tf_op jit(solution)/shard_map/all_to_all | solution.py:33
  329.2 224.2 %reduce-scatter.2.cloned.1.call-start = ((), (), s32[]{:S(2)}) async-start(), calls=%async_computation.6 | async-start | bytes 2162688 | tf_op jit(solution)/shard_map/reduce_scatter | solution.py:95
  372.4 4.8 copy-start.3
  386.4 4.9 copy-start.14
  386.4 168.5 %copy-start.1 = (bf16[1,1024,1024]{2,1,0:T(8,128)(2,1)S(1)}, bf16[1,1024,1024]{2,1,0:T(8,128)(2,1)}, u32[]{:S(2)}) copy-start(bf16[1,1024,1024]{2,1,0:T(8,128)(2,1)} %param.9) | copy-start | bytes 6291460
Sparse Core Ops, SparseCore 0:
  144.1 65.2 all-reduce.2
  333.8 219.5 reduce-scatter.1
where the time goes:
time: 568 us; the launch traced here: 562 us
  waiting for transfers between devices  294 us (52%)
  blocking collectives  97.2 us (17%)
  local copies, waits for them, and re-layouts  76.2 us (13%)
  matrix products  37.4 us (7%)
  other arithmetic  23 us (4%)
  starting transfers between devices  19.1 us (3%)
  between operations  14.4 us (3%)
    reduce_scatter x1, waiting for transfers between devices, on_device(): lax.psum_scatter(mix_term.astype(jnp.bfloat16), 'lat', scatter_dimension=...  161 us
    psum x1, waiting for transfers between devices, level_total(): return lax.psum(partial_value, 'lev')  65.4 us
    psum x1, blocking collectives, level_total(): return lax.psum(partial_value, 'lev')  52.7 us
    all_to_all x1, waiting for transfers between devices, to_columns(): return lax.all_to_all(block, 'lat', split_axis=2, concat_axis=1, tiled=True)  37.6 us
    all_to_all x1, waiting for transfers between devices, to_bands(): return lax.all_to_all(block, 'lat', split_axis=1, concat_axis=2, tiled=True)  30.3 us
    all_to_all x1, blocking collectives, to_columns(): return lax.all_to_all(block, 'lat', split_axis=2, concat_axis=1, tiled=True)  23.9 us
    all_to_all x1, blocking collectives, to_bands(): return lax.all_to_all(block, 'lat', split_axis=1, concat_axis=2, tiled=True)  20.6 us
    another operation x8, local copies, waits for them, and re-layouts  15.5 us
  transfers between devices with their start and end apart: 4, of which 4 were waited for; matrix products, arithmetic and copies ran while one was open for 6% of the time, Pallas kernels for 0%

commit v1 on v0

v1 whole, which is shorter than its diff:
```python
import functools
import math
from types import SimpleNamespace

import jax
import jax.numpy as jnp
from jax import lax
from jax.experimental import pallas as pl
from jax.experimental.pallas import tpu as pltpu
from jax.sharding import PartitionSpec as P

HEAD = 64
QUAD = 256
X_CHIPS = 4
epsilon = 1e-06
score_scale = 0.25
f32 = jnp.float32
bf16 = jnp.bfloat16
MESH = pl.DeviceIdType.MESH


def dot(a, b):
    return lax.dot_general(a, b, (((1,), (0,)), ((), ())), preferred_element_type=f32)


def dot_nt(a, b):
    return lax.dot_general(a, b, (((1,), (1,)), ((), ())), preferred_element_type=f32)


def dot_tn(a, b):
    return lax.dot_general(a, b, (((0,), (0,)), ((), ())), preferred_element_type=f32)


def log2(n):
    return n.bit_length() - 1


def lat_to_block(d, a):
    j = a >> log2(d.m)
    b = (a >> log2(d.rb * d.pl)) & (d.batch - 1)
    r = (a >> log2(d.pl)) & (d.rb - 1)
    p = a & (d.pl - 1)
    return (b * d.rb + r) * d.lon + j * d.pl + p


def block_to_group(d, c):
    b = c >> log2(d.pl * d.lat)
    p = (c >> log2(d.lat)) & (d.pl - 1)
    i = (c & (d.lat - 1)) >> log2(d.rb)
    r = c & (d.rb - 1)
    return i * d.m + b * d.rb * d.pl + r * d.pl + p


def permutation(d, index, forward):
    rows = lax.broadcasted_iota(jnp.int32, (d.tokens, d.tokens), 0)
    cols = lax.broadcasted_iota(jnp.int32, (d.tokens, d.tokens), 1)
    hit = index(d, rows) == cols if forward else index(d, cols) == rows
    return jnp.where(hit, 1.0, 0.0).astype(bf16)


def group_sum(values, ones):
    high = values.astype(bf16)
    low = (values - high.astype(f32)).astype(bf16)
    return dot(high, ones) + dot(low, ones)


def kernel(
    d,
    tok_hbm,
    mask_ref,
    wq_hbm,
    wm_hbm,
    scale_ref,
    cot_hbm,
    out_ref,
    dtok_ref,
    mg_ref,
    tok_v,
    cot_v,
    wq_v,
    wm_v,
    send_t,
    recv_t,
    send_f,
    recv_f,
    send_fa,
    recv_fa,
    flow_full,
    send_m,
    recv_m,
    send_ma,
    recv_ma,
    mix_full,
    send_d,
    recv_d,
    mg_s,
    recv_g1,
    send_g2,
    recv_g2,
    xg,
    rx_s,
    normed_s,
    raw_s,
    fac_s,
    qkv_s,
    attn_s,
    att_s,
    flow_a,
    flow_g,
    gp_s,
    dn_s,
    maskf,
    load_sem,
    send_sem,
    recv_sem,
):
    me = lax.axis_index("lat")
    lv = lax.axis_index("lev")
    nl, nv, m, width, tokens = d.nl, d.nv, d.m, d.width, d.tokens
    piece = d.piece
    loads = [
        pltpu.make_async_copy(src, dst, load_sem.at[n])
        for n, (src, dst) in enumerate(
            ((tok_hbm, tok_v), (cot_hbm, cot_v), (wq_hbm, wq_v), (wm_hbm, wm_v))
        )
    ]
    for load in loads:
        load.start()

    barrier = pltpu.get_barrier_semaphore()

    def greet_lat(k, carry):
        pl.semaphore_signal(
            barrier, inc=1, device_id={"lat": lax.rem(me + k, nl)}, device_id_type=MESH
        )
        return carry

    def greet_lev(k, carry):
        pl.semaphore_signal(
            barrier, inc=1, device_id={"lev": lax.rem(lv + k, nv)}, device_id_type=MESH
        )
        return carry

    lax.fori_loop(1, nl, greet_lat, 0)
    lax.fori_loop(1, nv, greet_lev, 0)

    def lat_copy(src, dst, sem, peer):
        return pltpu.make_async_remote_copy(
            src_ref=src,
            dst_ref=dst,
            send_sem=send_sem.at[sem],
            recv_sem=recv_sem.at[sem],
            device_id={"lat": peer},
            device_id_type=MESH,
        )

    def lev_copy(src, dst, sem, peer):
        return pltpu.make_async_remote_copy(
            src_ref=src,
            dst_ref=dst,
            send_sem=send_sem.at[sem],
            recv_sem=recv_sem.at[sem],
            device_id={"lev": peer},
            device_id_type=MESH,
        )

    def all_to_all(send, recv, sem):
        def body(k, carry):
            peer = lax.rem(me + k, nl)
            lat_copy(send.at[peer], recv.at[me], sem, peer).start()
            return carry

        lax.fori_loop(1, nl, body, 0)
        recv[me] = send[me]

    def all_to_all_done(send, recv, sem):
        return lat_copy(
            send.at[pl.ds(0, nl - 1)], recv.at[pl.ds(0, nl - 1)], sem, lax.rem(me + 1, nl)
        )

    def lanes(index):
        return pl.ds(pl.multiple_of(index * piece, piece), piece)

    def level_scatter(send, recv, sem):
        def body(k, carry):
            peer = lax.rem(lv + k, nv)
            lev_copy(send.at[:, :, lanes(peer)], recv.at[k - 1], sem, peer).start()
            return carry

        lax.fori_loop(1, nv, body, 0)

    def level_sum(send, recv, sem):
        lev_copy(recv, recv, sem, lax.rem(lv + 1, nv)).wait_recv()
        total = send[:, :, lanes(lv)].astype(f32)
        for k in range(nv - 1):
            total = total + recv[k].astype(f32)
        return total

    def level_gather(block, full, sem):
        def body(k, carry):
            peer = lax.rem(lv + k, nv)
            lev_copy(block, full.at[:, :, lanes(lv)], sem, peer).start()
            return carry

        lax.fori_loop(1, nv, body, 0)
        full[:, :, lanes(lv)] = block[...]

    def flat(ref):
        return ref[...].astype(f32).reshape(tokens, width)

    def blocks(values):
        return values.reshape(nl, m, width).astype(bf16)

    to_block = permutation(d, lat_to_block, True)
    loads[0].wait()
    send_t[...] = blocks(dot(to_block, tok_v[...]))
    loads[1].wait()
    send_f[...] = blocks(scale_ref[...] * dot(to_block, cot_v[...]))

    pl.semaphore_wait(barrier, nl - 1 + nv - 1)
    all_to_all(send_t, recv_t, 0)
    level_scatter(send_f, recv_f, 1)

    valid = mask_ref[...].astype(f32)
    for b in range(d.batch):
        row = jnp.concatenate([valid[b : b + 1]] * (QUAD // HEAD), axis=1)
        maskf[pl.ds(b * d.pl * d.lat, d.pl * d.lat), :] = jnp.broadcast_to(
            row, (d.pl * d.lat, d.keys)
        )

    send_fa[...] = level_sum(send_f, recv_f, 1).astype(bf16)
    all_to_all(send_fa, recv_fa, 2)

    all_to_all_done(send_t, recv_t, 0).wait_recv()
    x_group = dot(permutation(d, block_to_group, True), flat(recv_t).astype(bf16))
    xg[...] = x_group.astype(bf16)
    factor = lax.rsqrt(jnp.mean(x_group * x_group, axis=-1, keepdims=True) + epsilon)
    rx_s[...] = jnp.broadcast_to(factor, rx_s.shape)
    normed_s[...] = (x_group * factor).astype(bf16)

    all_to_all_done(send_fa, recv_fa, 2).wait_recv()
    level_gather(recv_fa, flow_full, 3)

    def same(shape, row_size, col_size):
        rows = lax.broadcasted_iota(jnp.int32, shape, 0) >> log2(row_size)
        cols = lax.broadcasted_iota(jnp.int32, shape, 1) >> log2(col_size)
        return jnp.where(rows == cols, 1.0, 0.0)

    def ones_e():
        return same((QUAD, QUAD), HEAD, HEAD).astype(bf16)

    def ones_k():
        return same((d.keys, d.keys), d.lat, d.lat).astype(bf16)

    def expand(block, spread):
        return jnp.concatenate([block] * (QUAD // HEAD), axis=0) * spread

    def collapse(product, spread):
        picked = product * spread
        total = picked[: d.lat]
        for h in range(1, QUAD // HEAD):
            total = total + picked[h * d.lat : (h + 1) * d.lat]
        return total

    groups = [slice(g * d.lat, (g + 1) * d.lat) for g in range(d.groups)]

    def head_mean(values, ones):
        return group_sum(values, ones) * (1.0 / HEAD)

    loads[2].wait()

    def columns(n, part):
        return pl.ds(pl.multiple_of(part * width + n * QUAD, QUAD), QUAD)

    def key_columns(n):
        return pl.ds(pl.multiple_of(n * d.keys, d.keys), d.keys)

    def forward_quad(n, carry):
        ones = ones_e()
        spread = same((d.keys, QUAD), d.lat, HEAD).astype(bf16)
        normed = normed_s[...]
        cast = []
        for part in range(2):
            raw = dot(normed, wq_v[:, columns(n, part)])
            fac = lax.rsqrt(head_mean(raw * raw, ones) + epsilon)
            raw_s[:, columns(n, part)] = raw
            fac_s[:, columns(n, part)] = fac
            cast.append((raw * fac).astype(bf16))
            qkv_s[:, columns(n, part)] = cast[part]
        value = dot(normed, wq_v[:, columns(n, 2)]).astype(bf16)
        qkv_s[:, columns(n, 2)] = value
        query, key = cast
        scores = jnp.concatenate(
            [dot_nt(query[g], expand(key[g], spread)) for g in groups], axis=0
        )
        exp_scores = jnp.exp(scores * score_scale) * maskf[...]
        attn = exp_scores / group_sum(exp_scores, ones_k())
        attn_s[:, key_columns(n)] = attn
        attn_b = attn.astype(bf16)
        attended = jnp.concatenate(
            [dot(attn_b[g], expand(value[g], spread)) for g in groups], axis=0
        )
        att_s[:, columns(n, 0)] = attended.astype(bf16)
        return carry

    lax.fori_loop(0, d.quads, forward_quad, 0)

    att_s[...] = dot(permutation(d, block_to_group, False), att_s[...]).astype(bf16)
    loads[3].wait()
    send_m[...] = blocks(dot(att_s[...], wm_v[...]))
    level_scatter(send_m, recv_m, 4)

    lev_copy(recv_f, recv_f, 3, lax.rem(lv + 1, nv)).wait_recv()
    flow_a[...] = flat(flow_full).astype(bf16)

    def mix_rows(n, carry):
        rows = pl.ds(pl.multiple_of(n * QUAD, QUAD), QUAD)
        part = dot_tn(att_s[:, rows], flow_a[...]) * d.grad_scale
        per = QUAD // (d.nx * d.out_rows)
        mg_s[pl.ds(n * per, per)] = part.astype(bf16).reshape(per, d.nx, d.out_rows, width)
        return carry

    lax.fori_loop(0, d.quads, mix_rows, 0)

    z_at = me >> log2(d.nx)
    x_at = me & (d.nx - 1)

    def scatter_x(k, carry):
        x_to = (x_at + k) & (d.nx - 1)
        lat_copy(mg_s.at[:, x_to], recv_g1.at[k - 1], 5, z_at * d.nx + x_to).start()
        return carry

    lax.fori_loop(1, d.nx, scatter_x, 0)

    flow_g[...] = dot(permutation(d, block_to_group, True), flow_a[...]).astype(bf16)

    def backward_quad(n, carry):
        ones = ones_e()
        spread = same((d.keys, QUAD), d.lat, HEAD)
        spread_b = spread.astype(bf16)
        rows = pl.ds(pl.multiple_of(n * QUAD, QUAD), QUAD)
        d_att = dot_nt(flow_g[...], wm_v[rows, :]).astype(bf16)
        query = qkv_s[:, columns(n, 0)]
        key = qkv_s[:, columns(n, 1)]
        value = qkv_s[:, columns(n, 2)]
        attn = attn_s[:, key_columns(n)]
        attn_b = attn.astype(bf16)
        d_attn = jnp.concatenate(
            [dot_nt(d_att[g], expand(value[g], spread_b)) for g in groups], axis=0
        )
        inner = group_sum(attn * d_attn, ones_k())
        d_scores = (attn * (d_attn - inner) * score_scale).astype(bf16)
        d_value = jnp.concatenate(
            [collapse(dot_tn(attn_b[g], d_att[g]), spread) for g in groups], axis=0
        )
        d_key = jnp.concatenate(
            [collapse(dot_tn(d_scores[g], query[g]), spread) for g in groups], axis=0
        )
        d_query = jnp.concatenate(
            [dot(d_scores[g], expand(key[g], spread_b)) for g in groups], axis=0
        )
        gp_s[:, columns(n, 2)] = d_value.astype(bf16)
        for part, upstream in ((0, d_query), (1, d_key)):
            up = upstream.astype(bf16).astype(f32)
            raw = raw_s[:, columns(n, part)]
            fac = fac_s[:, columns(n, part)]
            mean = head_mean(up * raw, ones)
            gp_s[:, columns(n, part)] = (fac * up - raw * (fac * fac * fac) * mean).astype(bf16)
        return carry

    half = d.quads // 2
    lax.fori_loop(0, half, backward_quad, 0)

    send_ma[...] = level_sum(send_m, recv_m, 4).astype(bf16)
    all_to_all(send_ma, recv_ma, 6)

    lax.fori_loop(half, d.quads, backward_quad, 0)

    all_to_all_done(send_ma, recv_ma, 6).wait_recv()
    level_gather(recv_ma, mix_full, 7)

    def project_back(n, carry):
        cols = pl.ds(pl.multiple_of(n * QUAD, QUAD), QUAD)
        dn_s[:, cols] = dot_nt(gp_s[...], wq_v[cols, :])
        return carry

    lax.fori_loop(0, d.quads, project_back, 0)

    x_group = xg[...].astype(f32)
    d_normed = dn_s[...]
    factor = rx_s[:, :1]
    mean = jnp.mean(d_normed * x_group, axis=-1, keepdims=True)
    d_group = (factor * d_normed - x_group * (factor * factor * factor * mean)).astype(bf16)
    send_d[...] = blocks(dot(permutation(d, block_to_group, False), d_group))
    all_to_all(send_d, recv_d, 8)

    lat_copy(recv_g1, recv_g1, 5, z_at * d.nx + ((x_at + 1) & (d.nx - 1))).wait_recv()

    def sum_x(n, carry):
        total = mg_s[n, x_at].astype(f32)
        for k in range(d.nx - 1):
            total = total + recv_g1[k, n].astype(f32)
        send_g2[n] = total.astype(bf16)
        return carry

    lax.fori_loop(0, d.nz, sum_x, 0)

    def scatter_z(k, carry):
        z_to = (z_at + k) & (d.nz - 1)
        lat_copy(send_g2.at[z_to], recv_g2.at[k - 1], 9, z_to * d.nx + x_at).start()
        return carry

    lax.fori_loop(1, d.nz, scatter_z, 0)

    to_lat = permutation(d, lat_to_block, False)
    lev_copy(recv_m, recv_m, 7, lax.rem(lv + 1, nv)).wait_recv()
    mixed = (flat(send_t) + scale_ref[...] * flat(mix_full)).astype(bf16)
    out_ref[...] = dot(to_lat, mixed).astype(bf16)

    all_to_all_done(send_d, recv_d, 8).wait_recv()
    d_lat = dot(to_lat, flat(recv_d).astype(bf16))
    dtok_ref[...] = (cot_v[...].astype(f32) + d_lat).astype(bf16)

    z_peer = ((z_at + 1) & (d.nz - 1)) * d.nx + x_at
    lat_copy(recv_g2, recv_g2, 9, z_peer).wait_recv()
    total = send_g2[z_at].astype(f32)
    for k in range(d.nz - 1):
        total = total + recv_g2[k].astype(f32)
    mg_ref[...] = total

    for send, recv, sem in (
        (send_t, recv_t, 0),
        (send_fa, recv_fa, 2),
        (send_ma, recv_ma, 6),
        (send_d, recv_d, 8),
    ):
        all_to_all_done(send, recv, sem).wait_send()
    lev_peer = lax.rem(lv + 1, nv)
    for ref, sem in ((recv_f, 1), (recv_f, 3), (recv_m, 4), (recv_m, 7)):
        lev_copy(ref, ref, sem, lev_peer).wait_send()
    lat_copy(recv_g1, recv_g1, 5, z_peer).wait_send()
    lat_copy(recv_g2, recv_g2, 9, z_peer).wait_send()


def on_device(x_chips, tokens, key_mask, w_qkv, w_mix, level_scale, cotangent):
    batch, _, band_rows, lon, width = tokens.shape
    nl, nv = lax.axis_size("lat"), lax.axis_size("lev")
    d = SimpleNamespace(
        nl=nl, nv=nv, batch=batch, rb=band_rows, lon=lon, width=width, pl=lon // nl,
        lat=nl * band_rows, tokens=batch * band_rows * lon, piece=width // nv,
        nx=x_chips, nz=nl // x_chips, quads=width // QUAD, out_rows=width // nl,
    )
    d.m = d.tokens // nl
    d.groups = batch * d.pl
    d.keys = (QUAD // HEAD) * d.lat
    d.grad_scale = 1.0 / math.sqrt(batch * d.lat * lon)
    flat_shape = (d.tokens, width)
    block = (nl, d.m, width)
    part = (nl, d.m, d.piece)
    parts = (nv - 1,) + part

    def vmem(shape, dtype=bf16):
        return pltpu.VMEM(shape, dtype)

    scratch = [
        vmem(flat_shape),
        vmem(flat_shape),
        vmem((width, 3 * width)),
        vmem((width, width)),
        vmem(block),
        vmem(block),
        vmem(block),
        vmem(parts),
        vmem(part),
        vmem(part),
        vmem(block),
        vmem(block),
        vmem(parts),
        vmem(part),
        vmem(part),
        vmem(block),
        vmem(block),
        vmem(block),
        vmem((d.nz, d.nx, d.out_rows, width)),
        vmem((d.nx - 1, d.nz, d.out_rows, width)),
        vmem((d.nz, d.out_rows, width)),
        vmem((d.nz - 1, d.out_rows, width)),
        vmem(flat_shape),
        vmem((d.tokens, 128), f32),
        vmem(flat_shape),
        vmem((d.tokens, 2 * width), f32),
        vmem((d.tokens, 2 * width), f32),
        vmem((d.tokens, 3 * width)),
        vmem((d.tokens, d.quads * d.keys), f32),
        vmem(flat_shape),
        vmem(flat_shape),
        vmem(flat_shape),
        vmem((d.tokens, 3 * width)),
        vmem(flat_shape, f32),
        vmem((d.tokens, d.keys), f32),
        pltpu.SemaphoreType.DMA((4,)),
        pltpu.SemaphoreType.DMA((10,)),
        pltpu.SemaphoreType.DMA((10,)),
    ]
    any_space = pl.BlockSpec(memory_space=pl.ANY)
    in_vmem = pl.BlockSpec(memory_space=pltpu.VMEM)
    output, d_tokens, mix_grad = pl.pallas_call(
        functools.partial(kernel, d),
        name="latitude_block",
        out_shape=(
            jax.ShapeDtypeStruct(flat_shape, bf16),
            jax.ShapeDtypeStruct(flat_shape, bf16),
            jax.ShapeDtypeStruct((d.out_rows, width), f32),
        ),
        in_specs=[any_space, in_vmem, any_space, any_space, in_vmem, any_space],
        out_specs=(in_vmem, in_vmem, in_vmem),
        scratch_shapes=scratch,
        compiler_params=pltpu.CompilerParams(
            collective_id=0, has_side_effects=True, vmem_limit_bytes=60 * 1024 * 1024
        ),
    )(
        tokens.reshape(flat_shape),
        key_mask,
        w_qkv,
        w_mix.reshape(width, width),
        level_scale,
        cotangent.reshape(flat_shape),
    )
    return (
        output.reshape(tokens.shape),
        d_tokens.reshape(tokens.shape),
        mix_grad.reshape(1, d.out_rows, width),
    )


def solution(mesh, x_chips=X_CHIPS):
    return jax.shard_map(
        functools.partial(on_device, x_chips),
        mesh=mesh,
        in_specs=(
            P(None, "lev", "lat", None, None),
            P(),
            P(),
            P("lev", None, None),
            P("lev", None),
            P(None, "lev", "lat", None, None),
        ),
        out_specs=(
            P(None, "lev", "lat", None, None),
            P(None, "lev", "lat", None, None),
            P("lev", "lat", None),
        ),
        check_vma=False,
    )
```

time: 568 us -> 97.7 us (0.17); the launches traced: 562 us -> 97.5 us
  waiting for transfers between devices: 294 us -> 0 us
  blocking collectives: 97.2 us -> 0 us
  Pallas kernels: 0 us -> 91.5 us
  local copies, waits for them, and re-layouts: 76.2 us -> 5.3 us
  matrix products: 37.4 us -> 0 us
  other arithmetic: 23 us -> 0 us
  starting transfers between devices: 19.1 us -> 0 us
  between operations: 14.4 us -> 0.64 us
    reduce_scatter x1 -> x0, waiting for transfers between devices: 161 us -> none  [on_device(): lax.psum_scatter(mix_term.astype(jnp.bfloat16), 'lat', scatter_dimension=...]
    pallas_call x0 -> x1, Pallas kernels: none -> 91.5 us  [on_device(): pl.pallas_call(functools.partial(kernel, d), name='latitude_block', out_s...]
    all_to_all x2 -> x0, waiting for transfers between devices: 67.9 us -> none  [the longest x1 37.6 us: to_columns(): return lax.all_to_all(block, 'lat', split_axis=2, concat_axis=1, tiled=True)]
    psum x1 -> x0, waiting for transfers between devices: 65.4 us -> none  [level_total(): return lax.psum(partial_value, 'lev')]
    psum x1 -> x0, blocking collectives: 52.7 us -> none  [level_total(): return lax.psum(partial_value, 'lev')]
    all_to_all x2 -> x0, blocking collectives: 44.5 us -> none  [the longest x1 23.9 us: to_columns(): return lax.all_to_all(block, 'lat', split_axis=2, concat_axis=1, tiled=True)]
    dot_general x11 -> x0, matrix products: 37.4 us -> none  [the longest x1 6.08 us: on_device(): jnp.einsum('blgpik,blkgpe->bligpe', d_scores_b, key_use, preferred_elemen...]
    all_to_all x2 -> x0, starting transfers between devices: 18.5 us -> none  [the longest x1 12.1 us: to_columns(): return lax.all_to_all(block, 'lat', split_axis=2, concat_axis=1, tiled=True)]
  transfers between devices with their start and end apart: 4 -> 0, of which waited for: 4 -> 0; matrix products, arithmetic and copies ran while one was open for 6% -> 0% of each run, Pallas kernels for 0% -> 0%
where the time goes in v1:
time: 97.7 us; the launch traced here: 97.5 us
  Pallas kernels  91.5 us (94%)
  local copies, waits for them, and re-layouts  5.3 us (5%)
    pallas_call x1, Pallas kernels, on_device(): pl.pallas_call(functools.partial(kernel, d), name='latitude_block', out_s...  91.5 us
    unnamed x3, local copies, waits for them, and re-layouts  5.3 us

profile of v1, /device:TPU:1, one launch (start us, length us, event | category | flops | bytes accessed | tf_op | source)
XLA Modules:
  0.0 97.5 jit_solution(14761113336498733685)
XLA Ops:
  0.6 91.5 %latitude_block.1 = (bf16[256,1024]{1,0:T(8,128)(2,1)}, bf16[256,1024]{1,0:T(8,128)(2,1)}, f32[32,1024]{1,0:T(8,128)}) custom-call(bf16[256,1024]{1,0:T(8,128)(2,1)} %bitcast.11, s32[2,64]{1,0:T(2,128)} %mask_ref.1, bf16[1024,3072]{1,0:T(8,128)(2,1)} %wq_hbm.1, bf16[1024,1024]{1,0:T(8,128)(2,1)} %bitcast.10, f32[1,1024]{1,0:T(1,128)} %scale_ref.1, ...), custom_call_target="tpu_custom_call" | custom-call | tf_op jit(solution)/shard_map/latitude_block/pallas_call | solution.py:507
  92.2 1.9 %copy.14 = bf16[2,1,2,64,1024]{4,3,2,1,0:T(8,128)(2,1)} copy(bf16[2,1,2,64,1024]{4,3,2,1,0:T(8,128)(2,1)} %bitcast.14) | data formatting | bytes 1048576
  94.1 1.9 %copy.15 = bf16[2,1,2,64,1024]{4,3,2,1,0:T(8,128)(2,1)} copy(bf16[2,1,2,64,1024]{4,3,2,1,0:T(8,128)(2,1)} %bitcast.13) | data formatting | bytes 1048576
  95.9 1.6 %copy.16 = f32[1,32,1024]{2,1,0:T(8,128)} copy(f32[1,32,1024]{2,1,0:T(8,128)} %bitcast.15) | data formatting | bytes 262144

commit v2 on v1

--- a/solution.py
+++ b/solution.py
@@ -82,11 +82,15 @@
     send_t,
     recv_t,
     send_f,
+    recv_fp,
+    sum_f,
     recv_f,
     send_fa,
     recv_fa,
     flow_full,
     send_m,
+    recv_mp,
+    sum_m,
     recv_m,
     send_ma,
     recv_ma,
@@ -94,7 +98,8 @@
     send_d,
     recv_d,
     mg_s,
-    recv_g1,
+    recv_ga,
+    recv_gb,
     send_g2,
     recv_g2,
     xg,
@@ -117,6 +122,7 @@
     me = lax.axis_index("lat")
     lv = lax.axis_index("lev")
     nl, nv, m, width, tokens = d.nl, d.nv, d.m, d.width, d.tokens
+    ny = nv // 2
     piece = d.piece
     loads = [
         pltpu.make_async_copy(src, dst, load_sem.at[n])
@@ -135,21 +141,20 @@
         )
         return carry
 
-    def greet_lev(k, carry):
+    lax.fori_loop(1, nl, greet_lat, 0)
+    pl.semaphore_signal(barrier, inc=1, device_id={"lev": lv ^ 1}, device_id_type=MESH)
+    for k in range(1, ny):
+        y_to = ((lv >> 1) + k) & (ny - 1)
         pl.semaphore_signal(
-            barrier, inc=1, device_id={"lev": lax.rem(lv + k, nv)}, device_id_type=MESH
-        )
-        return carry
-
-    lax.fori_loop(1, nl, greet_lat, 0)
-    lax.fori_loop(1, nv, greet_lev, 0)
-
-    def lat_copy(src, dst, sem, peer):
+            barrier, inc=1, device_id={"lev": y_to * 2 + (lv & 1)}, device_id_type=MESH
+        )
+
+    def lat_copy(src, dst, sem, peer, recv=None):
         return pltpu.make_async_remote_copy(
             src_ref=src,
             dst_ref=dst,
             send_sem=send_sem.at[sem],
-            recv_sem=recv_sem.at[sem],
+            recv_sem=recv_sem.at[sem if recv is None else recv],
             device_id={"lat": peer},
             device_id_type=MESH,
         )
@@ -178,48 +183,63 @@
             send.at[pl.ds(0, nl - 1)], recv.at[pl.ds(0, nl - 1)], sem, lax.rem(me + 1, nl)
         )
 
-    def lanes(index):
-        return pl.ds(pl.multiple_of(index * piece, piece), piece)
-
-    def level_scatter(send, recv, sem):
-        def body(k, carry):
-            peer = lax.rem(lv + k, nv)
-            lev_copy(send.at[:, :, lanes(peer)], recv.at[k - 1], sem, peer).start()
-            return carry
-
-        lax.fori_loop(1, nv, body, 0)
-
-    def level_sum(send, recv, sem):
-        lev_copy(recv, recv, sem, lax.rem(lv + 1, nv)).wait_recv()
-        total = send[:, :, lanes(lv)].astype(f32)
-        for k in range(nv - 1):
+    y_at, core = lv >> 1, lv & 1
+    partner = lv ^ 1
+    own_piece = core * ny + y_at
+    mine, other = pl.ds(core * ny, ny), pl.ds((1 - core) * ny, ny)
+    next_y = ((y_at + 1) & (ny - 1)) * 2 + core
+
+    def scatter_pair(send, recv_p, sem):
+        lev_copy(send.at[other], recv_p, sem, partner).start()
+
+    def scatter_ring(send, recv_p, pair_sem, part_sum, recv, sem):
+        lev_copy(recv_p, recv_p, pair_sem, partner).wait_recv()
+        part_sum[...] = (send[mine].astype(f32) + recv_p[...].astype(f32)).astype(bf16)
+        for k in range(1, ny):
+            y_to = (y_at + k) & (ny - 1)
+            lev_copy(part_sum.at[y_to], recv.at[k - 1], sem, y_to * 2 + core).start()
+
+    def level_sum(part_sum, recv, sem):
+        lev_copy(recv, recv, sem, next_y).wait_recv()
+        total = part_sum[y_at].astype(f32)
+        for k in range(ny - 1):
             total = total + recv[k].astype(f32)
         return total
 
-    def level_gather(block, full, sem):
-        def body(k, carry):
-            peer = lax.rem(lv + k, nv)
-            lev_copy(block, full.at[:, :, lanes(lv)], sem, peer).start()
-            return carry
-
-        lax.fori_loop(1, nv, body, 0)
-        full[:, :, lanes(lv)] = block[...]
+    def gather_ring(block, full, sem):
+        for k in range(1, ny):
+            y_to = (y_at + k) & (ny - 1)
+            lev_copy(block, full.at[own_piece], sem, y_to * 2 + core).start()
+        full[own_piece] = block[...]
+
+    def gather_pair(full, recv, ring_sem, sem):
+        lev_copy(recv, recv, ring_sem, next_y).wait_recv()
+        lev_copy(full.at[mine], full.at[mine], sem, partner).start()
 
     def flat(ref):
         return ref[...].astype(f32).reshape(tokens, width)
 
     def blocks(values):
         return values.reshape(nl, m, width).astype(bf16)
+
+    def store_pieces(ref, values):
+        for q in range(nv):
+            part = values[:, q * piece : (q + 1) * piece]
+            ref[q] = part.reshape(nl, m, piece).astype(bf16)
+
+    def load_pieces(ref):
+        parts = [ref[q].astype(f32).reshape(tokens, piece) for q in range(nv)]
+        return jnp.concatenate(parts, axis=1)
 
     to_block = permutation(d, lat_to_block, True)
     loads[0].wait()
     send_t[...] = blocks(dot(to_block, tok_v[...]))
     loads[1].wait()
-    send_f[...] = blocks(scale_ref[...] * dot(to_block, cot_v[...]))
-
-    pl.semaphore_wait(barrier, nl - 1 + nv - 1)
+    store_pieces(send_f, scale_ref[...] * dot(to_block, cot_v[...]))
+
+    pl.semaphore_wait(barrier, nl - 1 + ny)
+    scatter_pair(send_f, recv_fp, 1)
     all_to_all(send_t, recv_t, 0)
-    level_scatter(send_f, recv_f, 1)
 
     valid = mask_ref[...].astype(f32)
     for b in range(d.batch):
@@ -228,7 +248,8 @@
             row, (d.pl * d.lat, d.keys)
         )
 
-    send_fa[...] = level_sum(send_f, recv_f, 1).astype(bf16)
+    scatter_ring(send_f, recv_fp, 1, sum_f, recv_f, 11)
+    send_fa[...] = level_sum(sum_f, recv_f, 11).astype(bf16)
     all_to_all(send_fa, recv_fa, 2)
 
     all_to_all_done(send_t, recv_t, 0).wait_recv()
@@ -239,7 +260,7 @@
     normed_s[...] = (x_group * factor).astype(bf16)
 
     all_to_all_done(send_fa, recv_fa, 2).wait_recv()
-    level_gather(recv_fa, flow_full, 3)
+    gather_ring(recv_fa, flow_full, 3)
 
     def same(shape, row_size, col_size):
         rows = lax.broadcasted_iota(jnp.int32, shape, 0) >> log2(row_size)
@@ -270,10 +291,11 @@
     loads[2].wait()
 
     def columns(n, part):
-        return pl.ds(pl.multiple_of(part * width + n * QUAD, QUAD), QUAD)
+        start = part * width + n * QUAD
+        return pl.ds(start if isinstance(n, int) else pl.multiple_of(start, QUAD), QUAD)
 
     def key_columns(n):
-        return pl.ds(pl.multiple_of(n * d.keys, d.keys), d.keys)
+        return pl.ds(n * d.keys if isinstance(n, int) else pl.multiple_of(n * d.keys, d.keys), d.keys)
 
     def forward_quad(n, carry):
         ones = ones_e()
@@ -303,34 +325,83 @@
         att_s[:, columns(n, 0)] = attended.astype(bf16)
         return carry
 
-    lax.fori_loop(0, d.quads, forward_quad, 0)
+    lax.fori_loop(0, d.quads // 2, forward_quad, 0)
+    gather_pair(flow_full, recv_f, 3, 12)
+    lax.fori_loop(d.quads // 2, d.quads, forward_quad, 0)
 
     att_s[...] = dot(permutation(d, block_to_group, False), att_s[...]).astype(bf16)
     loads[3].wait()
-    send_m[...] = blocks(dot(att_s[...], wm_v[...]))
-    level_scatter(send_m, recv_m, 4)
-
-    lev_copy(recv_f, recv_f, 3, lax.rem(lv + 1, nv)).wait_recv()
-    flow_a[...] = flat(flow_full).astype(bf16)
-
-    def mix_rows(n, carry):
-        rows = pl.ds(pl.multiple_of(n * QUAD, QUAD), QUAD)
-        part = dot_tn(att_s[:, rows], flow_a[...]) * d.grad_scale
-        per = QUAD // (d.nx * d.out_rows)
-        mg_s[pl.ds(n * per, per)] = part.astype(bf16).reshape(per, d.nx, d.out_rows, width)
-        return carry
-
-    lax.fori_loop(0, d.quads, mix_rows, 0)
+    store_pieces(send_m, dot(att_s[...], wm_v[...]))
+    scatter_pair(send_m, recv_mp, 4)
+
+    lev_copy(recv_fp, recv_fp, 12, partner).wait_recv()
+    flow_a[...] = load_pieces(flow_full).astype(bf16)
 
     z_at = me >> log2(d.nx)
     x_at = me & (d.nx - 1)
-
-    def scatter_x(k, carry):
-        x_to = (x_at + k) & (d.nx - 1)
-        lat_copy(mg_s.at[:, x_to], recv_g1.at[k - 1], 5, z_at * d.nx + x_to).start()
-        return carry
-
-    lax.fori_loop(1, d.nx, scatter_x, 0)
+    x_next, x_prev = (x_at + 1) & (d.nx - 1), (x_at - 1) & (d.nx - 1)
+    x_far = (x_at + 2) & (d.nx - 1)
+    half_rows = d.out_rows // 2
+    top, bottom = pl.ds(0, half_rows), pl.ds(half_rows, half_rows)
+    sides = ((x_next, top, 0), (x_prev, bottom, 1))
+    offsets = sorted(range(d.chunks), key=lambda o: -min(o, d.chunks - o))
+
+    def chunk_of(step):
+        return ((z_at >> log2(d.per)) + offsets[step]) & (d.chunks - 1)
+
+    def chunk_rows(step):
+        return pl.ds(chunk_of(step) * d.per, d.per)
+
+    def column(x):
+        return z_at * d.nx + x
+
+    def far_copy(step, x_to, rows, side):
+        return lat_copy(
+            mg_s.at[chunk_rows(step), x_far, rows], recv_ga.at[side, step], 5, column(x_to),
+            15 + side * d.chunks + step,
+        )
+
+    def near_copy(step, x_to, side):
+        return lat_copy(
+            mg_s.at[chunk_rows(step), x_to], recv_gb.at[side, step], 9, column(x_to),
+            15 + (2 + side) * d.chunks + step,
+        )
+
+    def mix_chunk(step):
+        start = pl.multiple_of(chunk_of(step) * QUAD, QUAD)
+        part = dot_tn(att_s[:, pl.ds(start, QUAD)], flow_a[...]) * d.grad_scale
+        mg_s[chunk_rows(step)] = part.astype(bf16).reshape(d.per, d.nx, d.out_rows, width)
+        for x_to, rows, side in sides:
+            far_copy(step, x_to, rows, side).start()
+
+    def relay_chunk(step):
+        for x_to, rows, side in sides:
+            far_copy(step, x_to, rows, side).wait_recv()
+            mine = mg_s[chunk_rows(step), x_to, rows].astype(f32)
+            mine = mine + recv_ga[side, step].astype(f32)
+            mg_s[chunk_rows(step), x_to, rows] = mine.astype(bf16)
+            near_copy(step, x_to, side).start()
+
+    def finish_chunk(step):
+        total = mg_s[chunk_rows(step), x_at].astype(f32)
+        for x_to, rows, side in sides:
+            near_copy(step, x_to, side).wait_recv()
+            total = total + recv_gb[side, step].astype(f32)
+        send_g2[chunk_rows(step)] = total.astype(bf16)
+        for n in range(d.per):
+            if offsets[step] == 0:
+                if n == 0:
+                    continue
+                z_to = z_at ^ n
+            else:
+                z_to = chunk_of(step) * d.per + n
+            slot = ((z_to - z_at) & (d.nz - 1)) - 1
+            lat_copy(send_g2.at[z_to], recv_g2.at[slot], 10, z_to * d.nx + x_at, 9).start()
+
+    for step in range(d.chunks):
+        if step == d.chunks // 2:
+            scatter_ring(send_m, recv_mp, 4, sum_m, recv_m, 13)
+        mix_chunk(step)
 
     flow_g[...] = dot(permutation(d, block_to_group, True), flow_a[...]).astype(bf16)
 
@@ -338,7 +409,7 @@
         ones = ones_e()
         spread = same((d.keys, QUAD), d.lat, HEAD)
         spread_b = spread.astype(bf16)
-        rows = pl.ds(pl.multiple_of(n * QUAD, QUAD), QUAD)
+        rows = columns(n, 0)
         d_att = dot_nt(flow_g[...], wm_v[rows, :]).astype(bf16)
         query = qkv_s[:, columns(n, 0)]
         key = qkv_s[:, columns(n, 1)]
@@ -368,16 +439,12 @@
             gp_s[:, columns(n, part)] = (fac * up - raw * (fac * fac * fac) * mean).astype(bf16)
         return carry
 
-    half = d.quads // 2
-    lax.fori_loop(0, half, backward_quad, 0)
-
-    send_ma[...] = level_sum(send_m, recv_m, 4).astype(bf16)
-    all_to_all(send_ma, recv_ma, 6)
-
-    lax.fori_loop(half, d.quads, backward_quad, 0)
-
-    all_to_all_done(send_ma, recv_ma, 6).wait_recv()
-    level_gather(recv_ma, mix_full, 7)
+    for n in range(d.quads):
+        if n == d.quads - 1:
+            send_ma[...] = level_sum(sum_m, recv_m, 13).astype(bf16)
+            all_to_all(send_ma, recv_ma, 6)
+        backward_quad(n, 0)
+        relay_chunk(n)
 
     def project_back(n, carry):
         cols = pl.ds(pl.multiple_of(n * QUAD, QUAD), QUAD)
@@ -394,27 +461,16 @@
     send_d[...] = blocks(dot(permutation(d, block_to_group, False), d_group))
     all_to_all(send_d, recv_d, 8)
 
-    lat_copy(recv_g1, recv_g1, 5, z_at * d.nx + ((x_at + 1) & (d.nx - 1))).wait_recv()
-
-    def sum_x(n, carry):
-        total = mg_s[n, x_at].astype(f32)
-        for k in range(d.nx - 1):
-            total = total + recv_g1[k, n].astype(f32)
-        send_g2[n] = total.astype(bf16)
-        return carry
-
-    lax.fori_loop(0, d.nz, sum_x, 0)
-
-    def scatter_z(k, carry):
-        z_to = (z_at + k) & (d.nz - 1)
-        lat_copy(send_g2.at[z_to], recv_g2.at[k - 1], 9, z_to * d.nx + x_at).start()
-        return carry
-
-    lax.fori_loop(1, d.nz, scatter_z, 0)
+    all_to_all_done(send_ma, recv_ma, 6).wait_recv()
+    gather_ring(recv_ma, mix_full, 7)
+    for step in range(d.chunks):
+        if step == d.chunks // 2:
+            gather_pair(mix_full, recv_m, 7, 14)
+        finish_chunk(step)
 
     to_lat = permutation(d, lat_to_block, False)
-    lev_copy(recv_m, recv_m, 7, lax.rem(lv + 1, nv)).wait_recv()
-    mixed = (flat(send_t) + scale_ref[...] * flat(mix_full)).astype(bf16)
+    lev_copy(recv_mp, recv_mp, 14, partner).wait_recv()
+    mixed = (flat(send_t) + scale_ref[...] * load_pieces(mix_full)).astype(bf16)
     out_ref[...] = dot(to_lat, mixed).astype(bf16)
 
     all_to_all_done(send_d, recv_d, 8).wait_recv()
@@ -422,7 +478,7 @@
     dtok_ref[...] = (cot_v[...].astype(f32) + d_lat).astype(bf16)
 
     z_peer = ((z_at + 1) & (d.nz - 1)) * d.nx + x_at
-    lat_copy(recv_g2, recv_g2, 9, z_peer).wait_recv()
+    lat_copy(recv_g2, recv_g2, 10, z_peer, 9).wait_recv()
     total = send_g2[z_at].astype(f32)
     for k in range(d.nz - 1):
         total = total + recv_g2[k].astype(f32)
@@ -435,11 +491,19 @@
         (send_d, recv_d, 8),
     ):
         all_to_all_done(send, recv, sem).wait_send()
-    lev_peer = lax.rem(lv + 1, nv)
-    for ref, sem in ((recv_f, 1), (recv_f, 3), (recv_m, 4), (recv_m, 7)):
-        lev_copy(ref, ref, sem, lev_peer).wait_send()
-    lat_copy(recv_g1, recv_g1, 5, z_peer).wait_send()
-    lat_copy(recv_g2, recv_g2, 9, z_peer).wait_send()
+    for pair_ref, ring_ref, sems in (
+        (recv_fp, recv_f, (1, 11, 3, 12)),
+        (recv_mp, recv_m, (4, 13, 7, 14)),
+    ):
+        for sem, ref in zip(sems, (pair_ref, ring_ref, ring_ref, pair_ref)):
+            lev_copy(ref, ref, sem, partner).wait_send()
+    for ref, sem in ((recv_ga, 5), (recv_gb, 9), (recv_g2, 10)):
+        lat_copy(ref, ref, sem, z_peer, 9).wait_send()
+
+
+def hand_over(*refs):
+    for src, dst in zip(refs[:3], refs[3:]):
+        dst[...] = src[...]
 
 
 def on_device(x_chips, tokens, key_mask, w_qkv, w_mix, level_scale, cotangent):
@@ -453,11 +517,15 @@
     d.m = d.tokens // nl
     d.groups = batch * d.pl
     d.keys = (QUAD // HEAD) * d.lat
+    d.per = QUAD // (d.nx * d.out_rows)
+    d.chunks = d.nz // d.per
     d.grad_scale = 1.0 / math.sqrt(batch * d.lat * lon)
     flat_shape = (d.tokens, width)
     block = (nl, d.m, width)
     part = (nl, d.m, d.piece)
-    parts = (nv - 1,) + part
+    half = (nv // 2,) + part
+    parts = (nv // 2 - 1,) + part
+    whole = (nv,) + part
 
     def vmem(shape, dtype=bf16):
         return pltpu.VMEM(shape, dtype)
@@ -469,20 +537,25 @@
         vmem((width, width)),
         vmem(block),
         vmem(block),
-        vmem(block),
+        vmem(whole),
+        vmem(half),
+        vmem(half),
         vmem(parts),
         vmem(part),
         vmem(part),
-        vmem(block),
-        vmem(block),
+        vmem(whole),
+        vmem(whole),
+        vmem(half),
+        vmem(half),
         vmem(parts),
         vmem(part),
         vmem(part),
-        vmem(block),
+        vmem(whole),
         vmem(block),
         vmem(block),
         vmem((d.nz, d.nx, d.out_rows, width)),
-        vmem((d.nx - 1, d.nz, d.out_rows, width)),
+        vmem((2, d.chunks, d.per, d.out_rows // 2, width)),
+        vmem((2, d.chunks, d.per, d.out_rows, width)),
         vmem((d.nz, d.out_rows, width)),
         vmem((d.nz - 1, d.out_rows, width)),
         vmem(flat_shape),
@@ -499,12 +572,12 @@
         vmem(flat_shape, f32),
         vmem((d.tokens, d.keys), f32),
         pltpu.SemaphoreType.DMA((4,)),
-        pltpu.SemaphoreType.DMA((10,)),
-        pltpu.SemaphoreType.DMA((10,)),
+        pltpu.SemaphoreType.DMA((15,)),
+        pltpu.SemaphoreType.DMA((15 + 4 * d.chunks,)),
     ]
     any_space = pl.BlockSpec(memory_space=pl.ANY)
     in_vmem = pl.BlockSpec(memory_space=pltpu.VMEM)
-    output, d_tokens, mix_grad = pl.pallas_call(
+    results = pl.pallas_call(
         functools.partial(kernel, d),
         name="latitude_block",
         out_shape=(
@@ -526,6 +599,13 @@
         level_scale,
         cotangent.reshape(flat_shape),
     )
+    output, d_tokens, mix_grad = pl.pallas_call(
+        hand_over,
+        name="hand_over",
+        out_shape=tuple(jax.ShapeDtypeStruct(x.shape, x.dtype) for x in results),
+        in_specs=[in_vmem] * 3,
+        out_specs=(in_vmem,) * 3,
+    )(*results)
     return (
         output.reshape(tokens.shape),
         d_tokens.reshape(tokens.shape),

time: 97.7 us -> 78.9 us (0.81)
  Pallas kernels: 91.5 us -> 78 us
  local copies, waits for them, and re-layouts: 5.3 us -> 0 us
    pallas_call x1, Pallas kernels: 91.5 us -> 75.7 us  [on_device(): pl.pallas_call(functools.partial(kernel, d), name='latitude_block', out_s...]
    unnamed x3 -> x0, local copies, waits for them, and re-layouts: 5.3 us -> none
    pallas_call x0 -> x1, Pallas kernels: none -> 2.26 us  [on_device(): pl.pallas_call(hand_over, name='hand_over', out_shape=tuple((jax.ShapeDty...]
where the time goes in v2:
time: 78.9 us; the launch traced here: 78.6 us
  Pallas kernels  78 us (99%)
    pallas_call x1, Pallas kernels, on_device(): pl.pallas_call(functools.partial(kernel, d), name='latitude_block', out_s...  75.7 us
    pallas_call x1, Pallas kernels, on_device(): pl.pallas_call(hand_over, name='hand_over', out_shape=tuple((jax.ShapeDty...  2.26 us

profile of v2, /device:TPU:1, one launch (start us, length us, event | category | flops | bytes accessed | tf_op | source)
XLA Modules:
  0.0 78.6 jit_solution(7481380986802874451)
XLA Ops:
  0.6 75.7 %latitude_block.1 = (bf16[256,1024]{1,0:T(8,128)(2,1)}, bf16[256,1024]{1,0:T(8,128)(2,1)}, f32[32,1024]{1,0:T(8,128)}) custom-call(bf16[256,1024]{1,0:T(8,128)(2,1)} %bitcast.11, s32[2,64]{1,0:T(2,128)} %mask_ref.1, bf16[1024,3072]{1,0:T(8,128)(2,1)} %wq_hbm.1, bf16[1024,1024]{1,0:T(8,128)(2,1)} %bitcast.10, f32[1,1024]{1,0:T(1,128)} %scale_ref.1, ...), custom_call_target="tpu_custom_call" | custom-call | tf_op jit(solution)/shard_map/latitude_block/pallas_call | solution.py:580
  76.4 2.3 %hand_over.1 = (bf16[256,1024]{1,0:T(8,128)(2,1)}, bf16[256,1024]{1,0:T(8,128)(2,1)}, f32[32,1024]{1,0:T(8,128)}) custom-call(bf16[256,1024]{1,0:T(8,128)(2,1)} %get-tuple-element.9.refs_0_, bf16[256,1024]{1,0:T(8,128)(2,1)} %get-tuple-element.10.refs_1_, f32[32,1024]{1,0:T(8,128)} %get-tuple-element.11.refs_2_), custom_call_target="tpu_custom_call" | custom-call | tf_op jit(solution)/shard_map/hand_over/pallas_call | solution.py:602

commit v3 on v2

--- a/solution.py
+++ b/solution.py
@@ -59,9 +59,7 @@
 
 
 def group_sum(values, ones):
-    high = values.astype(bf16)
-    low = (values - high.astype(f32)).astype(bf16)
-    return dot(high, ones) + dot(low, ones)
+    return dot(values.astype(bf16), ones)
 
 
 def kernel(
@@ -291,13 +289,12 @@
     loads[2].wait()
 
     def columns(n, part):
-        start = part * width + n * QUAD
-        return pl.ds(start if isinstance(n, int) else pl.multiple_of(start, QUAD), QUAD)
+        return pl.ds(part * width + n * QUAD, QUAD)
 
     def key_columns(n):
-        return pl.ds(n * d.keys if isinstance(n, int) else pl.multiple_of(n * d.keys, d.keys), d.keys)
-
-    def forward_quad(n, carry):
+        return pl.ds(n * d.keys, d.keys)
+
+    def forward_quad(n):
         ones = ones_e()
         spread = same((d.keys, QUAD), d.lat, HEAD).astype(bf16)
         normed = normed_s[...]
@@ -323,17 +320,14 @@
             [dot(attn_b[g], expand(value[g], spread)) for g in groups], axis=0
         )
         att_s[:, columns(n, 0)] = attended.astype(bf16)
-        return carry
-
-    lax.fori_loop(0, d.quads // 2, forward_quad, 0)
-    gather_pair(flow_full, recv_f, 3, 12)
-    lax.fori_loop(d.quads // 2, d.quads, forward_quad, 0)
+
+    for n in range(d.quads):
+        if n == d.quads - 1:
+            gather_pair(flow_full, recv_f, 3, 12)
+        forward_quad(n)
 
     att_s[...] = dot(permutation(d, block_to_group, False), att_s[...]).astype(bf16)
     loads[3].wait()
-    store_pieces(send_m, dot(att_s[...], wm_v[...]))
-    scatter_pair(send_m, recv_mp, 4)
-
     lev_copy(recv_fp, recv_fp, 12, partner).wait_recv()
     flow_a[...] = load_pieces(flow_full).astype(bf16)
 
@@ -344,68 +338,91 @@
     half_rows = d.out_rows // 2
     top, bottom = pl.ds(0, half_rows), pl.ds(half_rows, half_rows)
     sides = ((x_next, top, 0), (x_prev, bottom, 1))
-    offsets = sorted(range(d.chunks), key=lambda o: -min(o, d.chunks - o))
-
-    def chunk_of(step):
-        return ((z_at >> log2(d.per)) + offsets[step]) & (d.chunks - 1)
-
-    def chunk_rows(step):
-        return pl.ds(chunk_of(step) * d.per, d.per)
+    reach = d.nz // 2
+    order = [reach] + [o for k in range(reach - 1, 0, -1) for o in (k, -k)] + [0]
+    z_next, z_prev = (z_at + 1) & (d.nz - 1), (z_at - 1) & (d.nz - 1)
+    x_sems = 15
+    z_sems = x_sems + 4 * d.chunks
+
+    def apart(offset):
+        return (z_at + offset) & (d.nz - 1)
+
+    def chunk_blocks(step):
+        return [(n, apart(order[step * d.per + n])) for n in range(d.per)]
 
     def column(x):
         return z_at * d.nx + x
 
-    def far_copy(step, x_to, rows, side):
-        return lat_copy(
-            mg_s.at[chunk_rows(step), x_far, rows], recv_ga.at[side, step], 5, column(x_to),
-            15 + side * d.chunks + step,
-        )
-
-    def near_copy(step, x_to, side):
-        return lat_copy(
-            mg_s.at[chunk_rows(step), x_to], recv_gb.at[side, step], 9, column(x_to),
-            15 + (2 + side) * d.chunks + step,
-        )
+    def far_copy(src, dst, x_to, step, side):
+        return lat_copy(src, dst, 5, column(x_to), x_sems + side * d.chunks + step)
+
+    def near_copy(src, dst, x_to, step, side):
+        return lat_copy(src, dst, 9, column(x_to), x_sems + (2 + side) * d.chunks + step)
 
     def mix_chunk(step):
-        start = pl.multiple_of(chunk_of(step) * QUAD, QUAD)
-        part = dot_tn(att_s[:, pl.ds(start, QUAD)], flow_a[...]) * d.grad_scale
-        mg_s[chunk_rows(step)] = part.astype(bf16).reshape(d.per, d.nx, d.out_rows, width)
+        for n, z in chunk_blocks(step):
+            cols = d.nx * d.out_rows
+            start = pl.multiple_of(z * cols, cols)
+            part = dot_tn(att_s[:, pl.ds(start, cols)], flow_a[...]) * d.grad_scale
+            mg_s[z] = part.reshape(d.nx, d.out_rows, width).astype(bf16)
         for x_to, rows, side in sides:
-            far_copy(step, x_to, rows, side).start()
+            for n, z in chunk_blocks(step):
+                far_copy(
+                    mg_s.at[z, x_far, rows], recv_ga.at[side, step, n], x_to, step, side
+                ).start()
 
     def relay_chunk(step):
         for x_to, rows, side in sides:
-            far_copy(step, x_to, rows, side).wait_recv()
-            mine = mg_s[chunk_rows(step), x_to, rows].astype(f32)
-            mine = mine + recv_ga[side, step].astype(f32)
-            mg_s[chunk_rows(step), x_to, rows] = mine.astype(bf16)
-            near_copy(step, x_to, side).start()
+            arrived = recv_ga.at[side, step]
+            far_copy(arrived, arrived, x_to, step, side).wait_recv()
+            for n, z in chunk_blocks(step):
+                mine = mg_s[z, x_to, rows].astype(f32) + recv_ga[side, step, n].astype(f32)
+                mg_s[z, x_to, rows] = mine.astype(bf16)
+                near_copy(
+                    mg_s.at[z, x_to], recv_gb.at[side, step, n], x_to, step, side
+                ).start()
+
+    def ring_copy(src, dst, side, step):
+        z_to = z_next if side == 0 else z_prev
+        send = 15 if step == 0 else 10
+        return lat_copy(src, dst, send, z_to * d.nx + x_at, z_sems + side * reach + step)
+
+    def ring_arrival(side, step):
+        slot = recv_g2.at[side, step, top] if step == 0 else recv_g2.at[side, step]
+        ring_copy(slot, slot, side, step).wait_recv()
+        if step == 0:
+            return (top if side == 0 else bottom), recv_g2[side, step, top].astype(f32)
+        return pl.ds(0, d.out_rows), recv_g2[side, step].astype(f32)
+
+    def ring_step(step):
+        for side in range(2):
+            z = apart((reach - step) * (1 if side == 0 else -1))
+            if step == 0:
+                rows = top if side == 0 else bottom
+                ring_copy(send_g2.at[z, rows], recv_g2.at[side, 0, top], side, 0).start()
+                continue
+            rows, value = ring_arrival(side, step - 1)
+            send_g2[z, rows] = (send_g2[z, rows].astype(f32) + value).astype(bf16)
+            ring_copy(send_g2.at[z], recv_g2.at[side, step], side, step).start()
 
     def finish_chunk(step):
-        total = mg_s[chunk_rows(step), x_at].astype(f32)
         for x_to, rows, side in sides:
-            near_copy(step, x_to, side).wait_recv()
-            total = total + recv_gb[side, step].astype(f32)
-        send_g2[chunk_rows(step)] = total.astype(bf16)
-        for n in range(d.per):
-            if offsets[step] == 0:
-                if n == 0:
-                    continue
-                z_to = z_at ^ n
-            else:
-                z_to = chunk_of(step) * d.per + n
-            slot = ((z_to - z_at) & (d.nz - 1)) - 1
-            lat_copy(send_g2.at[z_to], recv_g2.at[slot], 10, z_to * d.nx + x_at, 9).start()
+            arrived = recv_gb.at[side, step]
+            near_copy(arrived, arrived, x_to, step, side).wait_recv()
+        for n, z in chunk_blocks(step):
+            total = mg_s[z, x_at].astype(f32)
+            for side in range(2):
+                total = total + recv_gb[side, step, n].astype(f32)
+            send_g2[z] = total.astype(bf16)
+        if step < reach:
+            ring_step(step)
 
     for step in range(d.chunks):
-        if step == d.chunks // 2:
-            scatter_ring(send_m, recv_mp, 4, sum_m, recv_m, 13)
         mix_chunk(step)
 
     flow_g[...] = dot(permutation(d, block_to_group, True), flow_a[...]).astype(bf16)
 
-    def backward_quad(n, carry):
+    def backward_quad(n):
         ones = ones_e()
         spread = same((d.keys, QUAD), d.lat, HEAD)
         spread_b = spread.astype(bf16)
@@ -437,21 +454,32 @@
             fac = fac_s[:, columns(n, part)]
             mean = head_mean(up * raw, ones)
             gp_s[:, columns(n, part)] = (fac * up - raw * (fac * fac * fac) * mean).astype(bf16)
-        return carry
+
+    def project_back(n):
+        cols = columns(n, 0)
+        dn_s[:, cols] = dot_nt(gp_s[...], wq_v[cols, :])
+
+    def return_group(group):
+        far = reach - group
+        for offset in (far, 0 if group == 0 else -far):
+            z = apart(offset)
+            for k in range(offset == 0, d.nx):
+                peer = z * d.nx + ((x_at + k) & (d.nx - 1))
+                lat_copy(send_d.at[peer], recv_d.at[me], 8, peer).start()
 
     for n in range(d.quads):
+        backward_quad(n)
+        relay_chunk(n)
+        if n == 0:
+            store_pieces(send_m, dot(att_s[...], wm_v[...]))
+            scatter_pair(send_m, recv_mp, 4)
+        if n == 1:
+            scatter_ring(send_m, recv_mp, 4, sum_m, recv_m, 13)
+
+    for n in range(d.quads):
+        project_back(n)
         if n == d.quads - 1:
-            send_ma[...] = level_sum(sum_m, recv_m, 13).astype(bf16)
-            all_to_all(send_ma, recv_ma, 6)
-        backward_quad(n, 0)
-        relay_chunk(n)
-
-    def project_back(n, carry):
-        cols = pl.ds(pl.multiple_of(n * QUAD, QUAD), QUAD)
-        dn_s[:, cols] = dot_nt(gp_s[...], wq_v[cols, :])
-        return carry
-
-    lax.fori_loop(0, d.quads, project_back, 0)
+            finish_chunk(0)
 
     x_group = xg[...].astype(f32)
     d_normed = dn_s[...]
@@ -459,14 +487,19 @@
     mean = jnp.mean(d_normed * x_group, axis=-1, keepdims=True)
     d_group = (factor * d_normed - x_group * (factor * factor * factor * mean)).astype(bf16)
     send_d[...] = blocks(dot(permutation(d, block_to_group, False), d_group))
-    all_to_all(send_d, recv_d, 8)
-
-    all_to_all_done(send_ma, recv_ma, 6).wait_recv()
-    gather_ring(recv_ma, mix_full, 7)
-    for step in range(d.chunks):
-        if step == d.chunks // 2:
-            gather_pair(mix_full, recv_m, 7, 14)
+    send_ma[...] = level_sum(sum_m, recv_m, 13).astype(bf16)
+    all_to_all(send_ma, recv_ma, 6)
+    recv_d[me] = send_d[me]
+    return_group(0)
+
+    for step in range(1, d.chunks):
         finish_chunk(step)
+        if step < reach:
+            return_group(step)
+        if step == 2:
+            all_to_all_done(send_ma, recv_ma, 6).wait_recv()
+            gather_ring(recv_ma, mix_full, 7)
+    gather_pair(mix_full, recv_m, 7, 14)
 
     to_lat = permutation(d, lat_to_block, False)
     lev_copy(recv_mp, recv_mp, 14, partner).wait_recv()
@@ -477,12 +510,10 @@
     d_lat = dot(to_lat, flat(recv_d).astype(bf16))
     dtok_ref[...] = (cot_v[...].astype(f32) + d_lat).astype(bf16)
 
-    z_peer = ((z_at + 1) & (d.nz - 1)) * d.nx + x_at
-    lat_copy(recv_g2, recv_g2, 10, z_peer, 9).wait_recv()
-    total = send_g2[z_at].astype(f32)
-    for k in range(d.nz - 1):
-        total = total + recv_g2[k].astype(f32)
-    mg_ref[...] = total
+    mg_ref[...] = send_g2[z_at].astype(f32)
+    for side in range(2):
+        rows, value = ring_arrival(side, reach - 1)
+        mg_ref[rows, :] = mg_ref[rows, :] + value
 
     for send, recv, sem in (
         (send_t, recv_t, 0),
@@ -497,8 +528,11 @@
     ):
         for sem, ref in zip(sems, (pair_ref, ring_ref, ring_ref, pair_ref)):
             lev_copy(ref, ref, sem, partner).wait_send()
-    for ref, sem in ((recv_ga, 5), (recv_gb, 9), (recv_g2, 10)):
-        lat_copy(ref, ref, sem, z_peer, 9).wait_send()
+    sent = [(recv_ga, 5), (recv_gb, 9), (recv_g2.at[:, 0, top], 15)]
+    if reach > 1:
+        sent.append((recv_g2.at[:, pl.ds(1, reach - 1)], 10))
+    for ref, sem in sent:
+        lat_copy(ref, ref, sem, column(x_next), x_sems).wait_send()
 
 
 def hand_over(*refs):
@@ -557,7 +591,7 @@
         vmem((2, d.chunks, d.per, d.out_rows // 2, width)),
         vmem((2, d.chunks, d.per, d.out_rows, width)),
         vmem((d.nz, d.out_rows, width)),
-        vmem((d.nz - 1, d.out_rows, width)),
+        vmem((2, d.nz // 2, d.out_rows, width)),
         vmem(flat_shape),
         vmem((d.tokens, 128), f32),
         vmem(flat_shape),
@@ -572,8 +606,8 @@
         vmem(flat_shape, f32),
         vmem((d.tokens, d.keys), f32),
         pltpu.SemaphoreType.DMA((4,)),
-        pltpu.SemaphoreType.DMA((15,)),
-        pltpu.SemaphoreType.DMA((15 + 4 * d.chunks,)),
+        pltpu.SemaphoreType.DMA((16,)),
+        pltpu.SemaphoreType.DMA((15 + 4 * d.chunks + d.nz,)),
     ]
     any_space = pl.BlockSpec(memory_space=pl.ANY)
     in_vmem = pl.BlockSpec(memory_space=pltpu.VMEM)

time: 78.9 us -> 74 us (0.938)
  Pallas kernels: 78 us -> 73.2 us
    pallas_call x1, Pallas kernels: 75.7 us -> 71 us  [on_device(): pl.pallas_call(functools.partial(kernel, d), name='latitude_block', out_s...]
where the time goes in v3:
time: 74 us; the launch traced here: 73.8 us
  Pallas kernels  73.2 us (99%)
    pallas_call x1, Pallas kernels, on_device(): pl.pallas_call(functools.partial(kernel, d), name='latitude_block', out_s...  71 us
    pallas_call x1, Pallas kernels, on_device(): pl.pallas_call(hand_over, name='hand_over', out_shape=tuple((jax.ShapeDty...  2.26 us

profile of v3, /device:TPU:1, one launch (start us, length us, event | category | flops | bytes accessed | tf_op | source)
XLA Modules:
  0.0 73.8 jit_solution(18077022011459473033)
XLA Ops:
  0.6 71.0 %latitude_block.1 = (bf16[256,1024]{1,0:T(8,128)(2,1)}, bf16[256,1024]{1,0:T(8,128)(2,1)}, f32[32,1024]{1,0:T(8,128)}) custom-call(bf16[256,1024]{1,0:T(8,128)(2,1)} %bitcast.11, s32[2,64]{1,0:T(2,128)} %mask_ref.1, bf16[1024,3072]{1,0:T(8,128)(2,1)} %wq_hbm.1, bf16[1024,1024]{1,0:T(8,128)(2,1)} %bitcast.10, f32[1,1024]{1,0:T(1,128)} %scale_ref.1, ...), custom_call_target="tpu_custom_call" | custom-call | tf_op jit(solution)/shard_map/latitude_block/pallas_call | solution.py:614
  71.6 2.3 %hand_over.1 = (bf16[256,1024]{1,0:T(8,128)(2,1)}, bf16[256,1024]{1,0:T(8,128)(2,1)}, f32[32,1024]{1,0:T(8,128)}) custom-call(bf16[256,1024]{1,0:T(8,128)(2,1)} %get-tuple-element.9.refs_0_, bf16[256,1024]{1,0:T(8,128)(2,1)} %get-tuple-element.10.refs_1_, f32[32,1024]{1,0:T(8,128)} %get-tuple-element.11.refs_2_), custom_call_target="tpu_custom_call" | custom-call | tf_op jit(solution)/shard_map/hand_over/pallas_call | solution.py:636

commit v4 on v3

--- a/solution.py
+++ b/solution.py
@@ -108,7 +108,6 @@
     qkv_s,
     attn_s,
     att_s,
-    flow_a,
     flow_g,
     gp_s,
     dn_s,
@@ -237,7 +236,13 @@
 
     pl.semaphore_wait(barrier, nl - 1 + ny)
     scatter_pair(send_f, recv_fp, 1)
-    all_to_all(send_t, recv_t, 0)
+    z_here, x_here = me >> log2(d.nx), me & (d.nx - 1)
+    far_first = [d.nz // 2] + [o for k in range(d.nz // 2 - 1, 0, -1) for o in (k, -k)] + [0]
+    for offset in far_first:
+        for k in range(offset == 0, d.nx):
+            peer = ((z_here + offset) & (d.nz - 1)) * d.nx + ((x_here + k) & (d.nx - 1))
+            lat_copy(send_t.at[peer], recv_t.at[me], 0, peer).start()
+    recv_t[me] = send_t[me]
 
     valid = mask_ref[...].astype(f32)
     for b in range(d.batch):
@@ -326,10 +331,10 @@
             gather_pair(flow_full, recv_f, 3, 12)
         forward_quad(n)
 
-    att_s[...] = dot(permutation(d, block_to_group, False), att_s[...]).astype(bf16)
     loads[3].wait()
     lev_copy(recv_fp, recv_fp, 12, partner).wait_recv()
-    flow_a[...] = load_pieces(flow_full).astype(bf16)
+    flow_block = load_pieces(flow_full).astype(bf16)
+    flow_g[...] = dot(permutation(d, block_to_group, True), flow_block).astype(bf16)
 
     z_at = me >> log2(d.nx)
     x_at = me & (d.nx - 1)
@@ -363,7 +368,7 @@
         for n, z in chunk_blocks(step):
             cols = d.nx * d.out_rows
             start = pl.multiple_of(z * cols, cols)
-            part = dot_tn(att_s[:, pl.ds(start, cols)], flow_a[...]) * d.grad_scale
+            part = dot_tn(att_s[:, pl.ds(start, cols)], flow_g[...]) * d.grad_scale
             mg_s[z] = part.reshape(d.nx, d.out_rows, width).astype(bf16)
         for x_to, rows, side in sides:
             for n, z in chunk_blocks(step):
@@ -420,7 +425,6 @@
     for step in range(d.chunks):
         mix_chunk(step)
 
-    flow_g[...] = dot(permutation(d, block_to_group, True), flow_a[...]).astype(bf16)
 
     def backward_quad(n):
         ones = ones_e()
@@ -471,7 +475,8 @@
         backward_quad(n)
         relay_chunk(n)
         if n == 0:
-            store_pieces(send_m, dot(att_s[...], wm_v[...]))
+            att_block = dot(permutation(d, block_to_group, False), att_s[...])
+            store_pieces(send_m, dot(att_block.astype(bf16), wm_v[...]))
             scatter_pair(send_m, recv_mp, 4)
         if n == 1:
             scatter_ring(send_m, recv_mp, 4, sum_m, recv_m, 13)
@@ -493,9 +498,9 @@
     return_group(0)
 
     for step in range(1, d.chunks):
-        finish_chunk(step)
         if step < reach:
             return_group(step)
+        finish_chunk(step)
         if step == 2:
             all_to_all_done(send_ma, recv_ma, 6).wait_recv()
             gather_ring(recv_ma, mix_full, 7)
@@ -599,7 +604,6 @@
         vmem((d.tokens, 2 * width), f32),
         vmem((d.tokens, 3 * width)),
         vmem((d.tokens, d.quads * d.keys), f32),
-        vmem(flat_shape),
         vmem(flat_shape),
         vmem(flat_shape),
         vmem((d.tokens, 3 * width)),

time: 74 us -> 73.6 us (level)
  no operation moved by 1% of the time
where the time goes in v4:
time: 73.6 us; the launch traced here: 73.5 us
  Pallas kernels  72.9 us (99%)
    pallas_call x1, Pallas kernels, on_device(): pl.pallas_call(functools.partial(kernel, d), name='latitude_block', out_s...  70.6 us
    pallas_call x1, Pallas kernels, on_device(): pl.pallas_call(hand_over, name='hand_over', out_shape=tuple((jax.ShapeDty...  2.26 us

profile of v4, /device:TPU:1, one launch (start us, length us, event | category | flops | bytes accessed | tf_op | source)
XLA Modules:
  0.0 73.5 jit_solution(12283690373940058942)
XLA Ops:
  0.6 70.6 %latitude_block.1 = (bf16[256,1024]{1,0:T(8,128)(2,1)}, bf16[256,1024]{1,0:T(8,128)(2,1)}, f32[32,1024]{1,0:T(8,128)}) custom-call(bf16[256,1024]{1,0:T(8,128)(2,1)} %bitcast.11, s32[2,64]{1,0:T(2,128)} %mask_ref.1, bf16[1024,3072]{1,0:T(8,128)(2,1)} %wq_hbm.1, bf16[1024,1024]{1,0:T(8,128)(2,1)} %bitcast.10, f32[1,1024]{1,0:T(1,128)} %scale_ref.1, ...), custom_call_target="tpu_custom_call" | custom-call | tf_op jit(solution)/shard_map/latitude_block/pallas_call | solution.py:618
  71.3 2.3 %hand_over.1 = (bf16[256,1024]{1,0:T(8,128)(2,1)}, bf16[256,1024]{1,0:T(8,128)(2,1)}, f32[32,1024]{1,0:T(8,128)}) custom-call(bf16[256,1024]{1,0:T(8,128)(2,1)} %get-tuple-element.9.refs_0_, bf16[256,1024]{1,0:T(8,128)(2,1)} %get-tuple-element.10.refs_1_, f32[32,1024]{1,0:T(8,128)} %get-tuple-element.11.refs_2_), custom_call_target="tpu_custom_call" | custom-call | tf_op jit(solution)/shard_map/hand_over/pallas_call | solution.py:640
